TPU v7x, 512 devices: a whole 4x4x16 slice. The times are simulated.
512 devices in a mesh: row: 16 (over y, x), col: 16 (over z), depth: 2 (over core).
Axes of the slice: x: 4, y: 4, z: 16, core: 2. Of those that a mesh axis runs over, the one named last changes fastest.
Arguments:
- left_store: float32 [16, 2, 16, 2, 64, 1024], P('row', 'depth', 'col'), may hold values from -6 to 6
- left_home: int32 [16, 2, 16], P('row', 'depth'), may hold values from 0 to 15, each once within a row
- up_store: float32 [16, 2, 16, 2, 64, 1024], P('col', 'depth', 'row'), may hold values from -0.3125 to 0.3125
- up_home: int32 [16, 2, 16], P('col', 'depth'), may hold values from 0 to 15, each once within a row
- targets: int32 [16, 16, 2], P('row', 'col'), may hold values from 0 to 63, as said below
- sketch: float32 [16, 16, 2, 64, 1024], P('row', 'col'), may hold values from -0.1875 to 0.1875
Outputs:
- basis: float32 [16, 16, 2, 64, 1024], P('row', 'col', 'depth')
- weights: float32 [16, 16, 2, 64, 1024], P('row', 'col', 'depth')
Inputs may be any that keep to these rules, and one draw needn't show every extreme that they name: `left_home`: for each row and depth index the entries are the store positions 0 to 15, each once. `up_home`: for each col and depth index the entries are the store positions 0 to 15, each once. `targets`: the 2 entries of one row and col index are distinct.
All inputs are finite; a program needn't handle non-finite values.
Results may differ from a plain program's by a relative error of at most 0.0003.
Values sent between devices are 32-bit elements; how exact they have to be, the bound alone decides.
No kernel may reach another device: no remote copies, remote signals or barrier semaphores. Data moves between devices by JAX's collectives and lax.ppermute only.
A program may use at most 128 MiB of HBM per device.

v0:
```python
import math
import jax
import jax.numpy as jnp
from jax import lax
from jax.sharding import PartitionSpec as P

KD = 2
RB = 8
CB = 8


def split_up(shard, dim, devices):
    before, after = (shard.shape[:dim], shard.shape[dim + 1 :])
    return jnp.moveaxis(shard.reshape(*before, devices, -1, *after), dim, 0)


def sent_and_summed(shard, axis, dim):
    devices = lax.axis_size(axis)
    pieces = lax.all_to_all(split_up(shard, dim, devices), axis, 0, 0, tiled=True)
    return jnp.sum(pieces, axis=0)


def laid_out(pieces, dim):
    pieces = jnp.moveaxis(pieces, 0, dim)
    shape = pieces.shape
    return pieces.reshape(*shape[:dim], shape[dim] * shape[dim + 1], *shape[dim + 2 :])


def copy_for_each(shard, axis):
    devices = lax.axis_size(axis)
    return lax.all_to_all(
        jnp.broadcast_to(shard[None], (devices, *shard.shape)), axis, 0, 0, tiled=True
    )


def gathered_copies(shard, axis, dim):
    return laid_out(copy_for_each(shard, axis), dim)


def orthonormal(sample):
    gram_mat = jnp.einsum("pat,pbt->pab", sample, sample, precision=lax.Precision.HIGHEST)
    factor_low = jnp.linalg.cholesky(gram_mat)
    return lax.linalg.triangular_solve(factor_low, sample, left_side=True, lower=True)


def shards(left_store, left_home, up_store, up_home, targets, sketch):
    high = lax.Precision.HIGHEST
    left_local = left_store[0, 0]
    up_local = up_store[0, 0]
    left_table = left_home[0, 0]
    up_table = up_home[0, 0]
    left_all = lax.all_gather(left_local, "col", axis=0, tiled=True)
    up_all = lax.all_gather(up_local, "row", axis=0, tiled=True)
    left_pairs = jnp.take(left_all, left_table, axis=0)
    up_pairs = jnp.take(up_all, up_table, axis=0)
    chosen = targets[0, 0]
    block_row = chosen // CB
    block_col = chosen % CB
    row_pairs = jnp.take(left_pairs.reshape((RB, KD) + left_local.shape[1:]), block_row, axis=0)
    col_pairs = jnp.take(up_pairs.reshape((CB, KD) + up_local.shape[1:]), block_col, axis=0)
    row_basis = row_pairs[:, :, 0]
    row_coef = row_pairs[:, :, 1]
    col_coef = col_pairs[:, :, 0]
    col_basis = col_pairs[:, :, 1]
    test_rows = sketch[0, 0]
    middle = jnp.einsum("pkat,pkbt->pkab", row_coef, col_coef, precision=high)
    test_side = jnp.einsum("pat,pkbt->pkab", test_rows, col_basis, precision=high)
    folded = jnp.einsum("pkab,pkcb->pkac", test_side, middle, precision=high)
    sample_part = jnp.einsum("pkac,pkct->pat", folded, row_basis, precision=high)
    own_sketch = sent_and_summed(sample_part, "depth", 0)
    own_basis = orthonormal(own_sketch)
    bases = gathered_copies(own_basis, "depth", 0)
    inner_prod = jnp.einsum("pat,pkct->pkac", bases, row_basis, precision=high)
    turned = jnp.einsum("pkac,pkcb->pkab", inner_prod, middle, precision=high)
    project_part = jnp.einsum("pkab,pkbt->pat", turned, col_basis, precision=high)
    projected = sent_and_summed(project_part, "depth", 0)
    root_tile = math.sqrt(test_rows.shape[-1])
    return ((own_basis * root_tile)[None, None], (projected / root_tile)[None, None])


def solution(mesh):
    return jax.shard_map(
        shards,
        mesh=mesh,
        in_specs=(
            P("row", "depth", "col", None, None, None),
            P("row", "depth", None),
            P("col", "depth", "row", None, None, None),
            P("col", "depth", None),
            P("row", "col", None),
            P("row", "col", None, None, None),
        ),
        out_specs=(P("row", "col", "depth", None, None), P("row", "col", "depth", None, None)),
        check_vma=False,
    )
```

profile of v0, /device:TPU:1, one launch (start us, length us, event | category | flops | bytes accessed | tf_op | source)
XLA Modules:
  0.0 273.3 jit_solution(12288357249461976770)
XLA Ops:
  7.2 0.7 all-gather.7.cloned.1.call-update
  8.0 0.7 all-gather.5.cloned.1.call-update
  9.3 0.7 compare_and_fusion
  12.0 109.1 %all-gather.7.cloned.1.call-done = f32[16,1,1,2,64,1024]{5,4,3,2,1,0:T(8,128)} async-done(((f32[1,1,1,2,64,1024]{5,4,3,2,1,0:T(8,128)}), f32[16,1,1,2,64,1024]{5,4,3,2,1,0:T(8,128)}) %all-gather.7.cloned.1.call-update) | async-done | bytes 8388624 | tf_op jit(solution)/shard_map/all_gather | solution.py:52
  121.1 7.7 %gather_fusion.2 = f32[16,2,64,1024]{3,2,1,0:T(8,128)} fusion(f32[16,2,64,1024]{3,2,1,0:T(8,128)} %bitcast.97, s32[1024]{0:T(1024)S(1)} %pad_clamp_fusion.1), kind=kCustom, calls=%fused_computation.2.clone | custom fusion | bytes 16777280 | tf_op jit(solution)/shard_map/jit(_take)/gather | solution.py:54
  128.8 8.6 %broadcast_select_fusion = f32[16,2,64,1024]{3,2,1,0:T(8,128)} fusion(f32[16,2,64,1024]{3,2,1,0:T(8,128)} %gather_fusion.2, pred[16]{0:T(512)(128)(4,1)S(1)} %compare_and_fusion.1), kind=kLoop, calls=%fused_computation.4 | loop fusion | flops 2097152 | bytes 16777232 | tf_op jit(solution)/shard_map/jit(_take)/select_n | solution.py:54
  137.4 5.8 %gather_fusion.3 = f32[2,2,2,64,1024]{4,3,2,1,0:T(8,128)} fusion(f32[8,2,2,64,1024]{4,3,2,1,0:T(8,128)} %bitcast.94, s32[1024]{0:T(1024)S(1)} %pad_clamp_fusion), kind=kCustom, calls=%fused_computation.3.clone | custom fusion | bytes 4194312 | tf_op jit(solution)/shard_map/jit(_take)/gather | solution.py:59
  143.2 65.0 %all-gather.5.cloned.1.call-done = f32[16,1,1,2,64,1024]{5,4,3,2,1,0:T(8,128)} async-done(((f32[1,1,1,2,64,1024]{5,4,3,2,1,0:T(8,128)}), f32[16,1,1,2,64,1024]{5,4,3,2,1,0:T(8,128)}) %all-gather.5.cloned.1.call-update) | async-done | bytes 8388624 | tf_op jit(solution)/shard_map/all_gather | solution.py:53
  208.2 7.7 %gather_fusion = f32[16,2,64,1024]{3,2,1,0:T(8,128)} fusion(f32[16,2,64,1024]{3,2,1,0:T(8,128)} %bitcast.96, s32[1024]{0:T(1024)S(1)} %pad_clamp_fusion.3), kind=kCustom, calls=%fused_computation.clone | custom fusion | bytes 16777280 | tf_op jit(solution)/shard_map/jit(_take)/gather | solution.py:55
  215.8 8.6 %broadcast_select_fusion.1 = f32[16,2,64,1024]{3,2,1,0:T(8,128)} fusion(f32[16,2,64,1024]{3,2,1,0:T(8,128)} %gather_fusion, pred[16]{0:T(512)(128)(4,1)S(1)} %compare_and_fusion.3), kind=kLoop, calls=%fused_computation.5 | loop fusion | flops 2097152 | bytes 16777232 | tf_op jit(solution)/shard_map/jit(_take)/select_n | solution.py:55
  224.4 5.4 %gather_fusion.1 = f32[2,2,2,64,1024]{4,3,2,1,0:T(8,128)} fusion(f32[8,2,2,64,1024]{4,3,2,1,0:T(8,128)} %bitcast.95, s32[1024]{0:T(1024)S(1)} %pad_clamp_fusion.2), kind=kCustom, calls=%fused_computation.1.clone | custom fusion | bytes 4194312 | tf_op jit(solution)/shard_map/jit(_take)/gather | solution.py:60
  229.9 2.8 %copy_select_fusion = (f32[2,2,2,64,1024]{4,3,1,0,2:T(8,128)S(1)}, f32[2,2,2,64,1024]{4,3,1,0,2:T(8,128)S(1)}) fusion(f32[2,2,2,64,1024]{4,3,2,1,0:T(8,128)} %gather_fusion.3, pred[2]{0:T(512)(128)(4,1)S(1)} %get-tuple-element.4, f32[2,2,2,64,1024]{4,3,2,1,0:T(8,128)} %gather_fusion.1, pred[2]{0:T(512)(128)(4,1)S(1)} %get-tuple-element.8), kind=kLoop, calls=%fused_computation.6 | loop fusion | flops 1048576 | bytes 8388612 | tf_op jit(solution)/shard_map/jit(_take)/select_n | solution.py:59
  232.7 1.6 fusion.1
  234.3 1.1 fusion
  235.7 0.7 convolution_bitcast_fusion.1
  236.4 4.6 %all_to_all.15 = f32[2,1,64,1024]{3,2,1,0:T(8,128)S(1)} all-to-all(f32[2,1,64,1024]{3,2,1,0:T(8,128)S(1)} %convolution_bitcast_fusion.1), channel_id=1, replica_groups=mesh['row'=16,'col'=16,'depth'=2] {'depth'}, dimensions={0} | all-to-all | bytes 1048576 | tf_op jit(solution)/shard_map/all_to_all | solution.py:19
  241.5 5.8 %custom-call.7 = f32[1,64,64]{2,1,0:T(8,128)S(1)} custom-call(f32[1,64,64]{2,1,0:T(8,128)S(1)} %fusion.6), custom_call_target="Cholesky" | custom-call | tf_op jit(solution)/shard_map/jit(cholesky)/cholesky | solution.py:42
  248.7 4.9 %custom-call.8 = f32[1,1,64,64]{2,3,1,0:T(8,128)S(1)} custom-call(f32[1,1,64,64]{3,2,1,0:T(8,128)S(1)} %fusion.5), custom_call_target="InvertDiagBlocksLowerTriangular" | custom-call | tf_op jit(solution)/shard_map/triangular_solve | solution.py:43
  254.1 0.7 multiply_bitcast_fusion.1
  254.8 4.2 %all_to_all.16 = f32[2,1,64,1024]{3,2,1,0:T(8,128)S(1)} all-to-all(f32[2,1,64,1024]{3,2,1,0:T(8,128)S(1)} %broadcast_in_dim.33), channel_id=1, replica_groups=mesh['row'=16,'col'=16,'depth'=2] {'depth'}, dimensions={0} | all-to-all | bytes 1048576 | tf_op jit(solution)/shard_map/all_to_all | solution.py:31
  259.0 1.6 fusion.2
  260.9 0.7 convolution_bitcast_fusion
  261.6 4.2 %all_to_all.17 = f32[2,1,64,1024]{3,2,1,0:T(8,128)S(1)} all-to-all(f32[2,1,64,1024]{3,2,1,0:T(8,128)S(1)} %convolution_bitcast_fusion), channel_id=1, replica_groups=mesh['row'=16,'col'=16,'depth'=2] {'depth'}, dimensions={0} | all-to-all | bytes 1048576 | tf_op jit(solution)/shard_map/all_to_all | solution.py:19
  265.8 0.7 multiply_bitcast_fusion
  (28 shorter events, 5.7 us)
Async XLA Ops:
  7.2 225.5 %copy-start = (f32[1,1,2,64,1024]{4,3,2,1,0:T(8,128)S(1)}, f32[1,1,2,64,1024]{4,3,2,1,0:T(8,128)}, u32[]{:S(2)}) copy-start(f32[1,1,2,64,1024]{4,3,2,1,0:T(8,128)} %param.15) | copy-start | bytes 1572868
  7.2 113.9 %all-gather.7.cloned.1.call-start = ((), (), s32[]{:S(2)}) async-start(), calls=%async_computation.4 | async-start | bytes 8912896 | tf_op jit(solution)/shard_map/all_gather | solution.py:52
  7.9 200.3 %all-gather.5.cloned.1.call-start = ((), (), s32[]{:S(2)}) async-start(), calls=%async_computation.3 | async-start | bytes 8912896 | tf_op jit(solution)/shard_map/all_gather | solution.py:53
  232.6 3.1 %copy-start.1 = (f32[2,2,2,64,1024]{4,3,1,0,2:T(8,128)}, f32[2,2,2,64,1024]{4,3,1,0,2:T(8,128)S(1)}, u32[]{:S(2)}) copy-start(f32[2,2,2,64,1024]{4,3,1,0,2:T(8,128)S(1)} %get-tuple-element.10) | copy-start | bytes 6291460
  253.6 5.4 %copy-start.2 = (f32[2,2,2,64,1024]{4,3,1,0,2:T(8,128)S(1)}, f32[2,2,2,64,1024]{4,3,1,0,2:T(8,128)}, u32[]{:S(2)}) copy-start(f32[2,2,2,64,1024]{4,3,1,0,2:T(8,128)} %copy-done.1) | copy-start | bytes 6291460
Sparse Core Ops, SparseCore 0:
  10.1 110.9 all-gather.6
  124.1 84.0 all-gather.4
where the time goes:
time: 274 us; the launch traced here: 273 us
  waiting for transfers between devices  175 us (64%)
  other arithmetic  36.9 us (13%)
  local copies, waits for them, and re-layouts  26.7 us (10%)
  between operations  14.2 us (5%)
  blocking collectives  12.9 us (5%)
  matrix products  7.07 us (3%)
    all_gather x1, waiting for transfers between devices, shards(): left_all = lax.all_gather(left_local, 'col', axis=0, tiled=True)  109 us
    all_gather x1, waiting for transfers between devices, shards(): up_all = lax.all_gather(up_local, 'row', axis=0, tiled=True)  65 us
    select_n x2, other arithmetic, shards(): left_pairs = jnp.take(left_all, left_table, axis=0)  9.27 us
    select_n x2, other arithmetic, shards(): up_pairs = jnp.take(up_all, up_table, axis=0)  9.26 us
    all_to_all x2, blocking collectives, sent_and_summed(): lax.all_to_all(split_up(shard, dim, devices), axis, 0, 0, tiled=True)  8.78 us
    gather x1, local copies, waits for them, and re-layouts, shards(): left_pairs = jnp.take(left_all, left_table, axis=0)  7.68 us
    gather x1, local copies, waits for them, and re-layouts, shards(): up_pairs = jnp.take(up_all, up_table, axis=0)  7.67 us
    another operation x3, other arithmetic, orthonormal(): factor_low = jnp.linalg.cholesky(gram_mat)  6.52 us
  transfers between devices with their start and end apart: 2, of which 2 were waited for; matrix products, arithmetic and copies ran while one was open for 9% of the time, Pallas kernels for 0%

commit v1 on v0

--- a/solution.py
+++ b/solution.py
@@ -50,7 +50,11 @@
     left_table = left_home[0, 0]
     up_table = up_home[0, 0]
     left_all = lax.all_gather(left_local, "col", axis=0, tiled=True)
-    up_all = lax.all_gather(up_local, "row", axis=0, tiled=True)
+    peers = lax.axis_size("row")
+    repeats = [peers if d == 0 else 1 for d in range(up_local.ndim)]
+    up_all = lax.all_to_all(
+        jnp.tile(up_local, repeats), "row", split_axis=0, concat_axis=0, tiled=True
+    )
     left_pairs = jnp.take(left_all, left_table, axis=0)
     up_pairs = jnp.take(up_all, up_table, axis=0)
     chosen = targets[0, 0]

time: 274 us -> 232 us (0.85)
  waiting for transfers between devices: 175 us -> 117 us
  starting transfers between devices: 0.08 us -> 7.79 us
  local copies, waits for them, and re-layouts: 26.7 us -> 31.7 us
  blocking collectives: 12.9 us -> 16.9 us
  other arithmetic: 36.9 us -> 33.6 us
    all_to_all x0 -> x1, waiting for transfers between devices: none -> 117 us  [shards(): lax.all_to_all(jnp.tile(up_local, repeats), 'row', split_axis=0, concat_a...]
    all_gather x1, waiting for transfers between devices: 109 us -> 0.01 us  [shards(): left_all = lax.all_gather(left_local, 'col', axis=0, tiled=True)]
    all_gather x1 -> x0, waiting for transfers between devices: 65 us -> none  [shards(): up_all = lax.all_gather(up_local, 'row', axis=0, tiled=True)]
    all_to_all x0 -> x1, starting transfers between devices: none -> 7.76 us  [shards(): lax.all_to_all(jnp.tile(up_local, repeats), 'row', split_axis=0, concat_a...]
    another operation x0 -> x1, local copies, waits for them, and re-layouts: none -> 5.32 us  [shards(): jnp.tile(up_local, repeats)]
    all_to_all x2, blocking collectives: 8.78 us -> 12.7 us  [sent_and_summed(): lax.all_to_all(split_up(shard, dim, devices), axis, 0, 0, tiled=True)]
  transfers between devices with their start and end apart: 2 -> 2, of which waited for: 2 -> 1; matrix products, arithmetic and copies ran while one was open for 9% -> 12% of each run, Pallas kernels for 0% -> 0%
where the time goes in v1:
time: 232 us; the launch traced here: 229 us
  waiting for transfers between devices  117 us (50%)
  other arithmetic  33.6 us (14%)
  local copies, waits for them, and re-layouts  31.7 us (14%)
  blocking collectives  16.9 us (7%)
  between operations  14.3 us (6%)
  starting transfers between devices  7.79 us (3%)
  matrix products  7.07 us (3%)
    all_to_all x1, waiting for transfers between devices, shards(): lax.all_to_all(jnp.tile(up_local, repeats), 'row', split_axis=0, concat_a...  117 us
    all_to_all x2, blocking collectives, sent_and_summed(): lax.all_to_all(split_up(shard, dim, devices), axis, 0, 0, tiled=True)  12.7 us
    select_n x2, other arithmetic, shards(): left_pairs = jnp.take(left_all, left_table, axis=0)  8.61 us
    select_n x2, other arithmetic, shards(): up_pairs = jnp.take(up_all, up_table, axis=0)  8.61 us
    all_to_all x1, starting transfers between devices, shards(): lax.all_to_all(jnp.tile(up_local, repeats), 'row', split_axis=0, concat_a...  7.76 us
    gather x1, local copies, waits for them, and re-layouts, shards(): left_pairs = jnp.take(left_all, left_table, axis=0)  7.68 us
    gather x1, local copies, waits for them, and re-layouts, shards(): up_pairs = jnp.take(up_all, up_table, axis=0)  7.67 us
    another operation x3, other arithmetic, orthonormal(): factor_low = jnp.linalg.cholesky(gram_mat)  6.52 us
  transfers between devices with their start and end apart: 2, of which 1 were waited for; matrix products, arithmetic and copies ran while one was open for 12% of the time, Pallas kernels for 0%

profile of v1, /device:TPU:1, one launch (start us, length us, event | category | flops | bytes accessed | tf_op | source)
XLA Modules:
  0.0 228.8 jit_solution(11892628957496668006)
XLA Ops:
  7.2 0.7 all-gather.3.cloned.1.call-update
  7.9 5.3 %tile.9 = f32[16,2,64,1024]{3,2,1,0:T(8,128)} broadcast(f32[2,64,1024]{2,1,0:T(8,128)} %bitcast.97), dimensions={1,2,3} | broadcast | bytes 8912896 | tf_op jit(solution)/shard_map/tile | solution.py:56
  13.2 7.8 %all-to-all-start = ((f32[16,2,64,1024]{3,2,1,0:T(8,128)}), f32[16,2,64,1024]{3,2,1,0:T(8,128)}, u32[]{:S(2)}, u32[]{:S(2)}) async-start(f32[16,2,64,1024]{3,2,1,0:T(8,128)} %tile.9), calls=%async_computation | async-start | bytes 16777216 | tf_op jit(solution)/shard_map/all_to_all | solution.py:55
  21.2 116.8 %all-to-all-done = f32[16,2,64,1024]{3,2,1,0:T(8,128)} async-done(((f32[16,2,64,1024]{3,2,1,0:T(8,128)}), f32[16,2,64,1024]{3,2,1,0:T(8,128)}, u32[]{:S(2)}, u32[]{:S(2)}) %all-to-all-start) | async-done | bytes 8388640 | tf_op jit(solution)/shard_map/all_to_all | solution.py:55
  138.0 7.7 %gather_fusion = f32[16,2,64,1024]{3,2,1,0:T(8,128)} fusion(f32[16,2,64,1024]{3,2,1,0:T(8,128)} %all-to-all-done, s32[1024]{0:T(1024)S(1)} %pad_clamp_fusion.3), kind=kCustom, calls=%fused_computation.clone | custom fusion | bytes 16777280 | tf_op jit(solution)/shard_map/jit(_take)/gather | solution.py:59
  145.6 8.6 %broadcast_select_fusion.1 = f32[16,2,64,1024]{3,2,1,0:T(8,128)} fusion(f32[16,2,64,1024]{3,2,1,0:T(8,128)} %gather_fusion, pred[16]{0:T(512)(128)(4,1)S(1)} %compare_and_fusion.3), kind=kLoop, calls=%fused_computation.5 | loop fusion | flops 2097152 | bytes 16777232 | tf_op jit(solution)/shard_map/jit(_take)/select_n | solution.py:59
  154.3 5.4 %gather_fusion.1 = f32[2,2,2,64,1024]{4,3,2,1,0:T(8,128)} fusion(f32[8,2,2,64,1024]{4,3,2,1,0:T(8,128)} %bitcast.94, s32[1024]{0:T(1024)S(1)} %pad_clamp_fusion.2), kind=kCustom, calls=%fused_computation.1.clone | custom fusion | bytes 4194312 | tf_op jit(solution)/shard_map/jit(_take)/gather | solution.py:64
  159.7 7.7 %gather_fusion.2 = f32[16,2,64,1024]{3,2,1,0:T(8,128)} fusion(f32[16,2,64,1024]{3,2,1,0:T(8,128)} %bitcast.96, s32[1024]{0:T(1024)S(1)} %pad_clamp_fusion.1), kind=kCustom, calls=%fused_computation.2.clone | custom fusion | bytes 16777280 | tf_op jit(solution)/shard_map/jit(_take)/gather | solution.py:58
  167.4 8.6 %broadcast_select_fusion = f32[16,2,64,1024]{3,2,1,0:T(8,128)} fusion(f32[16,2,64,1024]{3,2,1,0:T(8,128)} %gather_fusion.2, pred[16]{0:T(512)(128)(4,1)S(1)} %compare_and_fusion.1), kind=kLoop, calls=%fused_computation.4 | loop fusion | flops 2097152 | bytes 16777232 | tf_op jit(solution)/shard_map/jit(_take)/select_n | solution.py:58
  176.0 5.4 %gather_fusion.3 = f32[2,2,2,64,1024]{4,3,2,1,0:T(8,128)} fusion(f32[8,2,2,64,1024]{4,3,2,1,0:T(8,128)} %bitcast.95, s32[1024]{0:T(1024)S(1)} %pad_clamp_fusion), kind=kCustom, calls=%fused_computation.3.clone | custom fusion | bytes 4194312 | tf_op jit(solution)/shard_map/jit(_take)/gather | solution.py:63
  181.4 2.8 %copy_select_fusion = (f32[2,2,2,64,1024]{4,3,1,0,2:T(8,128)S(1)}, f32[2,2,2,64,1024]{4,3,1,0,2:T(8,128)S(1)}) fusion(f32[2,2,2,64,1024]{4,3,2,1,0:T(8,128)} %gather_fusion.3, pred[2]{0:T(512)(128)(4,1)S(1)} %get-tuple-element.4, f32[2,2,2,64,1024]{4,3,2,1,0:T(8,128)} %gather_fusion.1, pred[2]{0:T(512)(128)(4,1)S(1)} %get-tuple-element.8), kind=kLoop, calls=%fused_computation.6 | loop fusion | flops 1048576 | bytes 8388612 | tf_op jit(solution)/shard_map/jit(_take)/select_n | solution.py:63
  184.2 1.1 fusion
  185.3 1.6 fusion.1
  187.2 0.7 convolution_bitcast_fusion.1
  187.9 8.6 %all_to_all.20 = f32[2,1,64,1024]{3,2,1,0:T(8,128)S(1)} all-to-all(f32[2,1,64,1024]{3,2,1,0:T(8,128)S(1)} %convolution_bitcast_fusion.1), channel_id=1, replica_groups=mesh['row'=16,'col'=16,'depth'=2] {'depth'}, dimensions={0} | all-to-all | bytes 1048576 | tf_op jit(solution)/shard_map/all_to_all | solution.py:19
  197.0 5.8 %custom-call.7 = f32[1,64,64]{2,1,0:T(8,128)S(1)} custom-call(f32[1,64,64]{2,1,0:T(8,128)S(1)} %fusion.6), custom_call_target="Cholesky" | custom-call | tf_op jit(solution)/shard_map/jit(cholesky)/cholesky | solution.py:42
  203.5 0.7 fusion.5
  204.2 4.9 %custom-call.8 = f32[1,1,64,64]{2,3,1,0:T(8,128)S(1)} custom-call(f32[1,1,64,64]{3,2,1,0:T(8,128)S(1)} %fusion.5), custom_call_target="InvertDiagBlocksLowerTriangular" | custom-call | tf_op jit(solution)/shard_map/triangular_solve | solution.py:43
  209.5 0.7 multiply_bitcast_fusion.1
  210.3 4.2 %all_to_all.21 = f32[2,1,64,1024]{3,2,1,0:T(8,128)S(1)} all-to-all(f32[2,1,64,1024]{3,2,1,0:T(8,128)S(1)} %broadcast_in_dim.33), channel_id=1, replica_groups=mesh['row'=16,'col'=16,'depth'=2] {'depth'}, dimensions={0} | all-to-all | bytes 1048576 | tf_op jit(solution)/shard_map/all_to_all | solution.py:31
  214.4 1.6 fusion.2
  216.3 0.7 convolution_bitcast_fusion
  217.0 4.2 %all_to_all.22 = f32[2,1,64,1024]{3,2,1,0:T(8,128)S(1)} all-to-all(f32[2,1,64,1024]{3,2,1,0:T(8,128)S(1)} %convolution_bitcast_fusion), channel_id=1, replica_groups=mesh['row'=16,'col'=16,'depth'=2] {'depth'}, dimensions={0} | all-to-all | bytes 1048576 | tf_op jit(solution)/shard_map/all_to_all | solution.py:19
  221.2 0.7 multiply_bitcast_fusion
  (34 shorter events, 2.4 us)
Async XLA Ops:
  7.2 178.1 %copy-start = (f32[1,1,2,64,1024]{4,3,2,1,0:T(8,128)S(1)}, f32[1,1,2,64,1024]{4,3,2,1,0:T(8,128)}, u32[]{:S(2)}) copy-start(f32[1,1,2,64,1024]{4,3,2,1,0:T(8,128)} %param.15) | copy-start | bytes 1572868
  7.2 152.5 %all-gather.3.cloned.1.call-start = ((), (), s32[]{:S(2)}) async-start(), calls=%async_computation.4 | async-start | bytes 8912896 | tf_op jit(solution)/shard_map/all_gather | solution.py:52
  13.2 7.8 %copy-start.3 = (s32[1,1,2]{2,1,0:T(1,128)S(1)}, s32[1,1,2]{2,1,0:T(1,128)}, u32[]{:S(2)}) copy-start(s32[1,1,2]{2,1,0:T(1,128)} %param.14) | copy-start | bytes 28
  13.2 7.8 %copy-start.4 = (s32[1,1,16]{2,1,0:T(1,128)S(1)}, s32[1,1,16]{2,1,0:T(1,128)}, u32[]{:S(2)}) copy-start(s32[1,1,16]{2,1,0:T(1,128)} %param.13) | copy-start | bytes 196
  13.2 7.9 %copy-start.5 = (s32[1,1,16]{2,1,0:T(1,128)S(1)}, s32[1,1,16]{2,1,0:T(1,128)}, u32[]{:S(2)}) copy-start(s32[1,1,16]{2,1,0:T(1,128)} %param.11) | copy-start | bytes 196
  13.2 124.7 %all-to-all-start = ((f32[16,2,64,1024]{3,2,1,0:T(8,128)}), f32[16,2,64,1024]{3,2,1,0:T(8,128)}, u32[]{:S(2)}, u32[]{:S(2)}) async-start(f32[16,2,64,1024]{3,2,1,0:T(8,128)} %tile.9), calls=%async_computation | async-start | bytes 16777216 | tf_op jit(solution)/shard_map/all_to_all | solution.py:55
  184.1 3.1 %copy-start.1 = (f32[2,2,2,64,1024]{4,3,1,0,2:T(8,128)}, f32[2,2,2,64,1024]{4,3,1,0,2:T(8,128)S(1)}, u32[]{:S(2)}) copy-start(f32[2,2,2,64,1024]{4,3,1,0,2:T(8,128)S(1)} %get-tuple-element.10) | copy-start | bytes 6291460
  209.1 5.4 %copy-start.2 = (f32[2,2,2,64,1024]{4,3,1,0,2:T(8,128)S(1)}, f32[2,2,2,64,1024]{4,3,1,0,2:T(8,128)}, u32[]{:S(2)}) copy-start(f32[2,2,2,64,1024]{4,3,1,0,2:T(8,128)} %copy-done.1) | copy-start | bytes 6291460
Sparse Core Ops, SparseCore 0:
  10.1 110.9 all-gather.2
